TPU v7x, 32 devices: a whole 2x2x4 slice. The times are simulated.
32 devices in a mesh: groups: 2 (over y), expert: 4 (over z), dp: 2 (over x), tile: 2 (over core).
Axes of the slice: x: 2, y: 2, z: 4, core: 2. Of those that a mesh axis runs over, the one named last changes fastest.
Arguments:
- features: bfloat16 [256, 1024], P(('groups', 'expert', 'dp', 'tile')), parts along dimension 0, may hold values from -6 to 6
- cross_weight: bfloat16 [1024, 1024], P(None, ('dp', 'tile')), may hold values from -0.1875 to 0.1875
- cross_bias: float32 [1024], replicated, may hold values from -1 to 1
- gate_weight: bfloat16 [1024, 36], replicated, may hold values from -24 to 24
- unit_experts: int32 [6, 6], replicated, may hold values from 0 to 15, all different within a row
- up_weight: bfloat16 [1024, 65536], P(None, ('expert', 'dp')), may hold values from -0.1875 to 0.1875
- up_bias: float32 [65536], P(('expert', 'dp')), may hold values from -3 to 3
- down_weight: bfloat16 [65536, 512], P(('expert', 'dp')), may hold values from -0.09375 to 0.09375
- down_bias: float32 [16, 512], replicated, may hold values from -3 to 3
- task_counts: int32 [32, 6], P(('groups', 'expert', 'dp', 'tile')), parts along dimension 0, may hold values from 1 to 8, as said below
- tower_in: bfloat16 [6, 512, 2048], P(None, None, ('dp', 'tile')), may hold values from -0.25 to 0.25
- tower_in_bias: float32 [6, 2048], P(None, ('dp', 'tile')), may hold values from -3 to 3
- tower_out: bfloat16 [6, 2048, 512], P(None, ('dp', 'tile')), may hold values from -0.125 to 0.125
- tower_out_bias: float32 [6, 512], replicated, may hold values from -3 to 3
Outputs:
- task_states: bfloat16 [256, 6, 512], P(('groups', 'expert', 'dp', 'tile')), parts along dimension 0
There are 2 independent parts, one for each index of `groups`. A program takes and returns all parts, laid end to end along the dimension named above; an argument that names none is the same for every part. Nothing has to cross between parts.
Inputs may be any that keep to these rules, and one draw needn't show every extreme that they name: `task_counts`: every task reaches a count of 8 on some row shard; which one is drawn from the seed.
All inputs are finite; a program needn't handle non-finite values.
Results may differ from a plain program's by a relative error of at most 0.0095.
Values may be sent and summed in bfloat16 or wider, within the bound.
A program may use at most 64 MiB of HBM per device.

v0:
```python
import jax
import jax.numpy as jnp
from jax import lax
from jax.sharding import PartitionSpec as P

EXPERT_FF = 4096


def body(
    features,
    cross_weight,
    cross_bias,
    gate_weight,
    unit_experts,
    up_weight,
    up_bias,
    down_weight,
    down_bias,
    task_counts,
    tower_in,
    tower_in_bias,
    tower_out,
    tower_out_bias,
):
    rows_own = features.shape[0]
    task_count = unit_experts.shape[0]
    unit_width = unit_experts.shape[1]
    out_width = down_weight.shape[1]
    column_base = features.astype(jnp.float32)
    scaled = (
        jnp.dot(
            features,
            lax.all_gather(cross_weight, ("dp", "tile"), axis=1, tiled=True),
            preferred_element_type=jnp.float32,
        )
        + cross_bias
    )
    crossed = (column_base * scaled + column_base).astype(jnp.bfloat16)
    logits = jnp.dot(features, gate_weight, preferred_element_type=jnp.float32)
    gate_probs = jax.nn.softmax(logits.reshape(rows_own, task_count, unit_width), axis=-1)
    hid_dev = up_weight.shape[1]
    pieces = max(1, hid_dev // EXPERT_FF)
    piece_width = hid_dev // pieces
    down_split = down_weight.reshape(pieces, piece_width, out_width)
    row_piece = lax.all_gather(crossed, ("expert", "dp"), axis=0, tiled=True)
    hidden = jnp.dot(row_piece, up_weight, preferred_element_type=jnp.float32) + up_bias
    hidden = (
        jax.nn.relu(hidden).astype(jnp.bfloat16).reshape(row_piece.shape[0], pieces, piece_width)
    )
    partial_value = jnp.einsum(
        "rpw,pwo->rpo", hidden, down_split, preferred_element_type=jnp.float32
    )
    expert_size = lax.axis_size("expert")
    data_size = lax.axis_size("dp")
    sources = expert_size * data_size
    blocks = partial_value.reshape(sources, rows_own, pieces, out_width)
    returned = lax.all_to_all(blocks, ("expert", "dp"), split_axis=0, concat_axis=0, tiled=True)
    per_expert = EXPERT_FF // piece_width
    ordered = jnp.moveaxis(returned, 2, 1).reshape(
        sources * pieces // per_expert, per_expert, rows_own, out_width
    )
    expert_out = jnp.sum(ordered, axis=1) + down_bias[:, None, :]
    onehot = (
        unit_experts[:, :, None] == jnp.arange(expert_out.shape[0], dtype=jnp.int32)[None, None, :]
    ).astype(jnp.float32)
    mix_weights = jnp.einsum("rtk,tke->rte", gate_probs, onehot)
    mixed_rows = jnp.einsum("rte,ero->rto", mix_weights, expert_out).astype(jnp.bfloat16)
    everyone = lax.all_gather(mixed_rows, ("dp", "tile"), axis=0, tiled=True)
    hidden = jnp.einsum("rto,toh->rth", everyone, tower_in, preferred_element_type=jnp.float32)
    hidden = jax.nn.relu(hidden + tower_in_bias[None, :, :]).astype(jnp.bfloat16)
    summed = lax.psum_scatter(
        jnp.einsum("rth,tho->rto", hidden, tower_out, preferred_element_type=jnp.float32),
        ("dp", "tile"),
        scatter_dimension=0,
        tiled=True,
    )
    tower_result = summed + tower_out_bias[None, :, :]
    position = jnp.arange(rows_own, dtype=jnp.int32)[:, None]
    active = position < task_counts
    return jnp.where(active[:, :, None], tower_result, 0.0).astype(jnp.bfloat16)


def solution(mesh):
    return jax.shard_map(
        body,
        mesh=mesh,
        in_specs=(
            P(("groups", "expert", "dp", "tile"), None),
            P(None, ("dp", "tile")),
            P(),
            P(),
            P(),
            P(None, ("expert", "dp")),
            P(("expert", "dp")),
            P(("expert", "dp"), None),
            P(),
            P(("groups", "expert", "dp", "tile"), None),
            P(None, None, ("dp", "tile")),
            P(None, ("dp", "tile")),
            P(None, ("dp", "tile"), None),
            P(),
        ),
        out_specs=P(("groups", "expert", "dp", "tile"), None, None),
        check_vma=False,
    )
```

profile of v0, /device:TPU:0, one launch (start us, length us, event | category | flops | bytes accessed | tf_op | source)
XLA Modules:
  0.0 128.5 jit_solution(7548105126115898000)
XLA Ops:
  6.5 0.0 copy-start
  6.5 0.0 all-gather.2.cloned.1.call-start
  6.5 0.7 all-gather.2.cloned.1.call-update
  7.3 1.3 fusion.21
  8.5 0.1 reshape.43
  8.6 25.9 %all-gather.2.cloned.1.call-done = bf16[1024,1024]{1,0:T(8,128)(2,1)} async-done(((bf16[1024,256]{1,0:T(8,128)(2,1)}), bf16[1024,1024]{1,0:T(8,128)(2,1)}) %all-gather.2.cloned.1.call-update) | async-done | bytes 2097168 | tf_op jit(solution)/shard_map/all_gather | solution.py:33
  34.5 2.1 %fusion.10 = bf16[8,1024]{1,0:T(8,128)(2,1)S(1)} fusion(bf16[8,1024]{1,0:T(8,128)(2,1)} %param.14, bf16[1024,1024]{1,0:T(8,128)(2,1)} %all-gather.2.cloned.1.call-done, f32[1024]{0:T(1024)} %param.16), kind=kOutput, calls=%fused_computation.16 | convolution fusion | flops 16818176 | bytes 2134016 | tf_op jit(solution)/shard_map/dot_general | solution.py:31
  36.6 30.6 %all_gather.10 = bf16[64,1024]{1,0:T(8,128)(2,1)S(1)} all-gather(bf16[8,1024]{1,0:T(8,128)(2,1)S(1)} %fusion.10), channel_id=1, replica_groups=mesh['groups'=2,'expert'=4,'dp'=2,'tile'=2] {'expert','dp'}, dimensions={0}, use_global_device_ids=true | all-gather | bytes 147456 | tf_op jit(solution)/shard_map/all_gather | solution.py:45
  67.2 8.9 %fusion.2 = bf16[64,8192]{1,0:T(8,128)(2,1)S(1)} fusion(bf16[64,1024]{1,0:T(8,128)(2,1)S(1)} %all_gather.10, bf16[1024,8192]{1,0:T(8,128)(2,1)} %param.19, f32[8192]{0:T(1024)} %param.20), kind=kOutput, calls=%fused_computation.3 | convolution fusion | flops 1075314688 | bytes 17989632 | tf_op jit(solution)/shard_map/dot_general | solution.py:46
  76.1 0.0 slice-done
  76.1 0.0 slice-done.1
  76.1 0.0 copy-start.4
  76.2 0.0 copy-start.1
  76.2 0.0 copy-start.2
  76.2 1.6 %convolution_bitcast_fusion.1 = f32[8,8,2,512]{3,1,0,2:T(8,128)S(1)} fusion(bf16[2,4096,512]{2,1,0:T(8,128)(2,1)S(1)} %bitcast.35, bf16[8,2,8,4096]{3,2,1,0:T(8,128)(2,1)S(1)} %bitcast.36), kind=kOutput, calls=%fused_computation.8 | convolution fusion | flops 536870912 | bytes 9699328 | tf_op jit(solution)/shard_map/rpw,pwo->rpo/dot_general | solution.py:50
  77.7 0.7 copy.20
  78.5 4.5 %all-to-all-start = ((f32[8,8,2,512]{3,1,2,0:T(8,128)}), f32[8,8,2,512]{3,1,2,0:T(8,128)S(1)}, u32[]{:S(2)}, u32[]{:S(2)}) async-start(f32[8,8,2,512]{3,1,2,0:T(8,128)} %copy.20), calls=%async_computation | async-start | bytes 524288 | tf_op jit(solution)/shard_map/all_to_all | solution.py:57
  83.0 0.0 reduce-scatter.2.cloned.1.call-start
  83.1 1.3 %fusion.20 = (f32[8,6]{1,0:T(8,128)S(1)}, f32[8,6,6]{2,1,0:T(8,128)S(1)}) fusion(f32[8,6,6]{2,1,0:T(8,128)S(1)} %reshape.43), kind=kOutput, calls=%fused_computation.32 | output fusion | flops 581 | bytes 2496 | tf_op jit(solution)/shard_map/sub | solution.py:40
  84.4 0.1 broadcast_divide_fusion
  84.5 0.2 convolution_bitcast_fusion.2
  84.7 6.5 %all-to-all-done = f32[8,8,2,512]{3,1,2,0:T(8,128)S(1)} async-done(((f32[8,8,2,512]{3,1,2,0:T(8,128)}), f32[8,8,2,512]{3,1,2,0:T(8,128)S(1)}, u32[]{:S(2)}, u32[]{:S(2)}) %all-to-all-start) | async-done | bytes 262176 | tf_op jit(solution)/shard_map/all_to_all | solution.py:57
  91.2 0.0 copy-done.1
  91.3 0.2 convolution_convert_fusion
  91.5 5.6 %all_gather.11 = bf16[32,6,512]{2,0,1:T(8,128)(2,1)S(1)} all-gather(bf16[8,6,512]{2,0,1:T(8,128)(2,1)S(1)} %copy.23), channel_id=1, replica_groups=mesh['groups'=2,'expert'=4,'dp'=2,'tile'=2] {'dp','tile'}, dimensions={0}, use_global_device_ids=true | all-gather | bytes 245760 | tf_op jit(solution)/shard_map/all_gather | solution.py:68
  97.1 0.0 copy-done.2
  97.1 3.8 %convolution_bitcast_fusion = f32[32,6,512]{2,0,1:T(8,128)} fusion(bf16[6,512,512]{2,1,0:T(8,128)(2,1)S(1)} %copy-done, bf16[32,6,512]{2,0,1:T(8,128)(2,1)S(1)} %all_gather.11, bf16[6,512,512]{2,1,0:T(8,128)(2,1)} %param.24, f32[6,512]{1,0:T(8,128)S(1)} %copy-done.2), kind=kOutput, calls=%fused_computation.4 | convolution fusion | flops 201621504 | bytes 6893568 | tf_op jit(solution)/shard_map/rth,tho->rto/dot_general | solution.py:72
  100.8 0.0 reduce-scatter.2.cloned.1.call-update
  100.9 0.0 copy-done.5
  100.9 0.1 iota_compare_fusion.2
  101.0 19.2 %reduce-scatter.2.cloned.1.call-done = f32[8,6,512]{2,0,1:T(8,128)} async-done(((f32[32,6,512]{2,0,1:T(8,128)}), f32[8,6,512]{2,0,1:T(8,128)}) %reduce-scatter.2.cloned.1.call-update) | async-done | bytes 98320 | tf_op jit(solution)/shard_map/reduce_scatter | solution.py:71
  120.1 1.6 %select_convert_fusion = bf16[8,6,512]{2,0,1:T(8,128)(2,1)} fusion(f32[8,6,512]{2,0,1:T(8,128)} %reduce-scatter.2.cloned.1.call-done, f32[6,512]{1,0:T(8,128)S(1)} %copy-done.3, pred[8,6]{0,1:T(8,128)(4,1)S(1)} %iota_compare_fusion.2), kind=kLoop, calls=%fused_computation.24 | loop fusion | flops 73728 | bytes 159792 | tf_op jit(solution)/shard_map/convert_element_type | solution.py:80
  (10 shorter events, 0.1 us)
Async XLA Ops:
  6.5 90.5 %copy-start = (bf16[6,512,512]{2,1,0:T(8,128)(2,1)S(1)}, bf16[6,512,512]{2,1,0:T(8,128)(2,1)}, u32[]{:S(2)}) copy-start(bf16[6,512,512]{2,1,0:T(8,128)(2,1)} %param.26) | copy-start | bytes 9437188
  6.5 27.9 %all-gather.2.cloned.1.call-start = ((), (), s32[]{:S(2)}) async-start(), calls=%async_computation.2 | async-start | bytes 2621440 | tf_op jit(solution)/shard_map/all_gather | solution.py:33
  34.5 41.7 %slice-start = ((s8[8388608]{0:T(1024)(128)(4,1)}), s8[4194304]{0:T(1024)(128)(4,1)S(1)}, s32[]{:S(2)}) async-start(s8[8388608]{0:T(1024)(128)(4,1)} %bitcast.33), calls=%async_computation.4 | async-start | bytes 8388608
  67.2 9.0 %slice-start.1 = ((s8[8388608]{0:T(1024)(128)(4,1)}), s8[4194304]{0:T(1024)(128)(4,1)S(1)}, s32[]{:S(2)}) async-start(s8[8388608]{0:T(1024)(128)(4,1)} %bitcast.33), calls=%async_computation.5 | async-start | bytes 8388608
  76.1 8.3 %copy-start.4 = (s32[6,6]{1,0:T(8,128)S(1)}, s32[6,6]{1,0:T(8,128)}, u32[]{:S(2)}) copy-start(s32[6,6]{1,0:T(8,128)} %param.18) | copy-start | bytes 436
  76.2 15.1 %copy-start.1 = (f32[16,512]{1,0:T(8,128)S(1)}, f32[16,512]{1,0:T(8,128)}, u32[]{:S(2)}) copy-start(f32[16,512]{1,0:T(8,128)} %param.22) | copy-start | bytes 98308
  76.2 20.9 %copy-start.2 = (f32[6,512]{1,0:T(8,128)S(1)}, f32[6,512]{1,0:T(8,128)}, u32[]{:S(2)}) copy-start(f32[6,512]{1,0:T(8,128)} %param.25) | copy-start | bytes 36868
  78.5 12.8 %all-to-all-start = ((f32[8,8,2,512]{3,1,2,0:T(8,128)}), f32[8,8,2,512]{3,1,2,0:T(8,128)S(1)}, u32[]{:S(2)}, u32[]{:S(2)}) async-start(f32[8,8,2,512]{3,1,2,0:T(8,128)} %copy.20), calls=%async_computation | async-start | bytes 524288 | tf_op jit(solution)/shard_map/all_to_all | solution.py:57
  83.0 37.1 %reduce-scatter.2.cloned.1.call-start = ((), (), s32[]{:S(2)}) async-start(), calls=%async_computation.3 | async-start | bytes 491520 | tf_op jit(solution)/shard_map/reduce_scatter | solution.py:71
  97.1 3.8 %copy-start.5 = (s32[1,6]{1,0:T(1,128)S(1)}, s32[1,6]{1,0:T(1,128)}, u32[]{:S(2)}) copy-start(s32[1,6]{1,0:T(1,128)} %param.23) | copy-start | bytes 76
  97.1 23.0 %copy-start.3 = (f32[6,512]{1,0:T(8,128)S(1)}, f32[6,512]{1,0:T(8,128)}, u32[]{:S(2)}) copy-start(f32[6,512]{1,0:T(8,128)} %param.27) | copy-start | bytes 36868
Sparse Core Ops, SparseCore 0:
  8.9 25.5 all-gather.1
  101.0 19.0 reduce-scatter.1
where the time goes:
time: 129 us
  waiting for transfers between devices  52.3 us (41%)
  blocking collectives  36.2 us (28%)
  matrix products  18 us (14%)
  between operations  13.5 us (10%)
  starting transfers between devices  4.57 us (4%)
  other arithmetic  3.11 us (2%)
    all_gather x1, blocking collectives, body(): row_piece = lax.all_gather(crossed, ('expert', 'dp'), axis=0, tiled=True)  30.6 us
    all_gather x1, waiting for transfers between devices, body(): lax.all_gather(cross_weight, ('dp', 'tile'), axis=1, tiled=True)  25.9 us
    reduce_scatter x1, waiting for transfers between devices, body(): lax.psum_scatter(jnp.einsum('rth,tho->rto', hidden, tower_out, preferred_...  19.2 us
    dot_general x1, matrix products, body(): jnp.dot(row_piece, up_weight, preferred_element_type=jnp.float32) + up_bias  8.94 us
    all_to_all x1, waiting for transfers between devices, body(): lax.all_to_all(blocks, ('expert', 'dp'), split_axis=0, concat_axis=0, til...  6.55 us
    all_gather x1, blocking collectives, body(): everyone = lax.all_gather(mixed_rows, ('dp', 'tile'), axis=0, tiled=True)  5.6 us
    all_to_all x1, starting transfers between devices, body(): lax.all_to_all(blocks, ('expert', 'dp'), split_axis=0, concat_axis=0, til...  4.53 us
    dot_general x1, matrix products, body(): jnp.einsum('rth,tho->rto', hidden, tower_out, preferred_element_type=jnp....  3.77 us
  transfers between devices with their start and end apart: 3, of which 3 were waited for; matrix products, arithmetic and copies ran while one was open for 2% of the time, Pallas kernels for 0%

commit v1 on v0

v1 whole, which is shorter than its diff:
```python
import functools

import jax
import jax.numpy as jnp
from jax import lax
from jax.experimental import pallas as pl
from jax.experimental.pallas import tpu as pltpu
from jax.sharding import PartitionSpec as P

EXPERT_FF = 4096
MESH = pl.DeviceIdType.MESH
F32 = jnp.float32
BF16 = jnp.bfloat16


def kernel(
    sizes,
    features,
    cross_weight,
    cross_bias,
    gate_weight,
    unit_experts,
    up_weight,
    up_bias,
    down_weight,
    down_bias,
    task_counts,
    tower_in,
    tower_in_bias,
    tower_out,
    tower_out_bias,
    out,
    feats,
    cross_v,
    cross_b,
    gate_v,
    up_v,
    up_b,
    down_v,
    down_b,
    tin_v,
    tin_b,
    tout_v,
    tout_b,
    rows_all,
    acc,
    sent,
    parts,
    mix_w,
    mixed,
    tower_own,
    tower_send,
    tower_recv,
    local_sem,
    f_send,
    f_recv,
    c_send,
    c_fwd,
    c_recv,
    e_send,
    e_recv,
    m_send,
    m_recv,
    t_send,
    t_recv,
):
    planes, dp_size, tile_size = sizes
    plane_devs = dp_size * tile_size
    chips = planes * dp_size
    ranks = chips * tile_size
    z, x, c = lax.axis_index("expert"), lax.axis_index("dp"), lax.axis_index("tile")
    chip = z * dp_size + x
    me = chip * tile_size + c
    spot = x * tile_size + c
    own = features.shape[0]
    width = features.shape[1]
    cols = cross_weight.shape[1]
    plane_rows = own * plane_devs
    tasks, unit_k = unit_experts.shape
    experts, out_w = down_bias.shape
    hid = up_v.shape[1]
    hid_base = pl.multiple_of(c * hid, 128)

    def rank_id(q):
        return {
            "expert": q // plane_devs,
            "dp": (q // tile_size) % dp_size,
            "tile": q % tile_size,
        }

    def plane_id(g):
        return {"dp": g // tile_size, "tile": g % tile_size}

    def loop(n, fn):
        lax.fori_loop(0, n, lambda i, _: (fn(i), 0)[1], 0)

    barrier = pltpu.get_barrier_semaphore()

    def greet(i):
        q = lax.rem(me + 1 + i, ranks)
        pl.semaphore_signal(barrier, inc=1, device_id=rank_id(q), device_id_type=MESH)

    loop(ranks - 1, greet)

    half = width // 2
    moves = [
        pltpu.make_async_copy(src, dst, local_sem.at[i])
        for i, (src, dst) in enumerate(
            [
                (features, feats.at[spot]),
                (cross_weight, cross_v),
                (cross_bias, cross_b),
                (gate_weight, gate_v),
                (up_bias, up_b),
                (down_bias, down_b),
                (tower_in_bias, tin_b),
                (tower_out_bias, tout_b),
                (up_weight.at[pl.ds(0, half), pl.ds(hid_base, hid)], up_v.at[pl.ds(0, half)]),
                (
                    up_weight.at[pl.ds(half, half), pl.ds(hid_base, hid)],
                    up_v.at[pl.ds(half, half)],
                ),
                (down_weight.at[pl.ds(hid_base, hid), :], down_v),
                (tower_in, tin_v),
                (tower_out, tout_v),
            ]
        )
    ]
    for move in moves:
        move.start()
    pl.semaphore_wait(barrier, ranks - 1)

    def row_copy(src_spot, to):
        return pltpu.make_async_remote_copy(
            src_ref=features,
            dst_ref=feats.at[src_spot],
            send_sem=f_send.at[to],
            recv_sem=f_recv.at[src_spot],
            device_id=plane_id(to),
            device_id_type=MESH,
        )

    def other(i):
        return lax.rem(spot + 1 + i, plane_devs)

    loop(plane_devs - 1, lambda i: row_copy(spot, other(i)).start())
    for move in moves[:4]:
        move.wait()
    loop(plane_devs - 1, lambda i: row_copy(other(i), spot).wait_recv())

    col_base = pl.multiple_of(spot * cols, 128)
    rows_f = feats[...].astype(F32).reshape(plane_rows, width)
    scaled = jnp.dot(rows_f.astype(BF16), cross_v[...], preferred_element_type=F32)
    scaled = scaled + cross_b[:, pl.ds(col_base, cols)]
    base = feats[:, :, pl.ds(col_base, cols)].astype(F32).reshape(plane_rows, cols)

    def region(q):
        r0 = pl.multiple_of((q // plane_devs) * plane_rows, plane_rows)
        c0 = pl.multiple_of(lax.rem(q, plane_devs) * cols, 128)
        return rows_all.at[pl.ds(r0, plane_rows), pl.ds(c0, cols)]

    region(me)[...] = (base * scaled + base).astype(BF16)

    def block_copy(q, to, sem):
        return pltpu.make_async_remote_copy(
            src_ref=region(q),
            dst_ref=region(q),
            send_sem=sem,
            recv_sem=c_recv.at[q],
            device_id=rank_id(to),
            device_id_type=MESH,
        )

    def other_chip(i):
        return lax.rem(chip + 1 + i, chips)

    def chip_send(i):
        k = other_chip(i)
        return block_copy(me, k * tile_size + c, c_send.at[k])

    def forward(k, j):
        t = lax.rem(c + j, tile_size)
        return block_copy(k * tile_size + c, chip * tile_size + t, c_fwd.at[k, t])

    loop(chips - 1, lambda i: chip_send(i).start())
    for j in range(1, tile_size):
        forward(chip, j).start()

    logits = jnp.dot(feats[spot], gate_v[...], preferred_element_type=F32)
    lane = lax.broadcasted_iota(jnp.int32, logits.shape, 1)
    probs = jnp.zeros_like(logits)
    picks = jnp.full(logits.shape, -1, jnp.int32)
    for t in range(tasks):
        group = (lane >= t * unit_k) & (lane < (t + 1) * unit_k)
        top = jnp.max(jnp.where(group, logits, -jnp.inf), axis=1, keepdims=True)
        powers = jnp.where(group, jnp.exp(jnp.where(group, logits - top, 0.0)), 0.0)
        probs = probs + powers / jnp.sum(powers, axis=1, keepdims=True)
        for k in range(unit_k):
            picks = jnp.where(lane == t * unit_k + k, unit_experts[t, k], picks)
    for t in range(tasks):
        group = (lane >= t * unit_k) & (lane < (t + 1) * unit_k)
        for e in range(experts):
            weight = jnp.sum(jnp.where(group & (picks == e), probs, 0.0), axis=1, keepdims=True)
            mix_w[t, e] = jnp.broadcast_to(weight, mix_w.shape[2:])

    def relay(i):
        k = lax.rem(chip + chips - 1 - i, chips)
        block_copy(k * tile_size + c, me, c_send.at[k]).wait_recv()
        for j in range(1, tile_size):
            forward(k, j).start()

    loop(chips - 1, relay)

    for move in moves[4:11]:
        move.wait()

    def late(i):
        k = lax.rem(chip + chips - i, chips)
        for j in range(1, tile_size):
            q = k * tile_size + lax.rem(c + j, tile_size)
            block_copy(q, me, c_send.at[k]).wait_recv()

    loop(chips, late)

    rows = planes * plane_rows
    block = min(128, rows)
    tn = min(512, hid)
    per_block = block // own

    def row_block(b):
        r0 = pl.multiple_of(b * block, block)
        acc[...] = jnp.zeros_like(acc)

        def unit_block(n):
            n0 = pl.multiple_of(n * tn, tn)
            h = jnp.dot(
                rows_all[pl.ds(r0, block), :], up_v[:, pl.ds(n0, tn)], preferred_element_type=F32
            )
            h = jnp.maximum(h + up_b[:, pl.ds(pl.multiple_of(hid_base + n0, 128), tn)], 0.0)
            acc[...] += jnp.dot(
                h.astype(BF16), down_v[pl.ds(n0, tn), :], preferred_element_type=F32
            )

        loop(hid // tn, unit_block)
        sent[pl.ds(b * per_block, per_block)] = (
            acc[...].reshape(per_block, own, out_w).astype(BF16)
        )

    loop(rows // block, row_block)

    def term_copy(src, to):
        return pltpu.make_async_remote_copy(
            src_ref=sent.at[to],
            dst_ref=parts.at[src],
            send_sem=e_send.at[to],
            recv_sem=e_recv.at[src],
            device_id=rank_id(to),
            device_id_type=MESH,
        )

    def other_rank(i):
        return lax.rem(me + 1 + i, ranks)

    loop(ranks - 1, lambda i: term_copy(me, other_rank(i)).start())
    parts[me] = sent[me]
    for move in moves[11:]:
        move.wait()
    loop(ranks - 1, lambda i: term_copy(other_rank(i), me).wait_recv())

    def mix_copy(src_spot, to, t):
        return pltpu.make_async_remote_copy(
            src_ref=mixed.at[src_spot, t],
            dst_ref=mixed.at[src_spot, t],
            send_sem=m_send.at[t, to],
            recv_sem=m_recv.at[t, src_spot],
            device_id=plane_id(to),
            device_id_type=MESH,
        )

    per_expert = ranks // experts
    for t in range(tasks):
        total = jnp.zeros((own, out_w), F32)
        for e in range(experts):
            value = jnp.broadcast_to(down_b[pl.ds(e, 1), :], (own, out_w))
            if per_expert <= 2:
                for i in range(per_expert):
                    value = value + parts[e * per_expert + i].astype(F32)
            else:
                value = lax.fori_loop(
                    0,
                    per_expert,
                    lambda i, v, e=e: v + parts[e * per_expert + i].astype(F32),
                    value,
                )
            weight = mix_w[t, e]
            total = total + jnp.concatenate([weight] * (out_w // weight.shape[1]), axis=1) * value
        mixed[spot, t] = total.astype(BF16)
        loop(plane_devs - 1, lambda i, t=t: mix_copy(spot, other(i), t).start())

    def tower_copy(src_spot, to, t):
        return pltpu.make_async_remote_copy(
            src_ref=tower_send.at[t, to],
            dst_ref=tower_recv.at[t, src_spot],
            send_sem=t_send.at[t, to],
            recv_sem=t_recv.at[t, src_spot],
            device_id=plane_id(to),
            device_id_type=MESH,
        )

    for t in range(tasks):
        loop(plane_devs - 1, lambda i, t=t: mix_copy(other(i), spot, t).wait_recv())
        m = mixed[:, t].astype(F32).reshape(plane_rows, out_w).astype(BF16)
        h = jnp.dot(m, tin_v[t], preferred_element_type=F32) + tin_b[pl.ds(t, 1), :]
        h = jnp.maximum(h, 0.0).astype(BF16)
        y = jnp.dot(h, tout_v[t], preferred_element_type=F32)
        y = y.reshape(plane_devs, own, out_w)
        tower_own[t] = y
        tower_send[t] = y.astype(BF16)
        loop(plane_devs - 1, lambda i, t=t: tower_copy(spot, other(i), t).start())

    position = lax.broadcasted_iota(jnp.int32, (own, out_w), 0)
    for t in range(tasks):
        loop(plane_devs - 1, lambda i, t=t: tower_copy(other(i), spot, t).wait_recv())
        tower_recv[t, spot] = jnp.zeros((own, out_w), BF16)
        value = tower_own[t, spot] + jnp.sum(tower_recv[t].astype(F32), axis=0)
        value = value + tout_b[pl.ds(t, 1), :]
        out[t] = jnp.where(position < task_counts[0, t], value, 0.0).astype(BF16)

    loop(plane_devs - 1, lambda i: row_copy(spot, other(i)).wait_send())
    loop(chips - 1, lambda i: chip_send(i).wait_send())

    def relayed(i):
        for j in range(1, tile_size):
            forward(lax.rem(chip + i, chips), j).wait_send()

    loop(chips, relayed)
    loop(ranks - 1, lambda i: term_copy(me, other_rank(i)).wait_send())
    for t in range(tasks):
        loop(plane_devs - 1, lambda i, t=t: mix_copy(spot, other(i), t).wait_send())
        loop(plane_devs - 1, lambda i, t=t: tower_copy(spot, other(i), t).wait_send())


def solution(mesh):
    shape = mesh.shape
    planes, dp_size, tile_size = shape["expert"], shape["dp"], shape["tile"]

    def body(*args):
        (features, cross_weight, cross_bias, gate_weight, unit_experts, up_weight, up_bias,
         down_weight, down_bias, task_counts, tower_in, tower_in_bias, tower_out,
         tower_out_bias) = args
        plane_devs = dp_size * tile_size
        chips = planes * dp_size
        ranks = chips * tile_size
        own, width = features.shape
        tasks = unit_experts.shape[0]
        experts, out_w = down_bias.shape
        hid = up_weight.shape[1] // tile_size
        assert EXPERT_FF % hid == 0
        rows = ranks * own
        dma = pltpu.SemaphoreType.DMA
        vmem = pltpu.VMEM
        hbm = pl.BlockSpec(memory_space=pltpu.MemorySpace.HBM)
        smem = pl.BlockSpec(memory_space=pltpu.MemorySpace.SMEM)
        in_specs = [hbm] * 14
        in_specs[4] = smem
        in_specs[9] = smem
        result = pl.pallas_call(
            functools.partial(kernel, (planes, dp_size, tile_size)),
            out_shape=jax.ShapeDtypeStruct((tasks, own, out_w), BF16),
            in_specs=in_specs,
            out_specs=pl.BlockSpec(memory_space=pltpu.VMEM),
            scratch_shapes=[
                vmem((plane_devs, own, width), BF16),
                vmem(cross_weight.shape, BF16),
                vmem((1, width), F32),
                vmem(gate_weight.shape, BF16),
                vmem((width, hid), BF16),
                vmem((1, up_bias.shape[0]), F32),
                vmem((hid, out_w), BF16),
                vmem(down_bias.shape, F32),
                vmem(tower_in.shape, BF16),
                vmem(tower_in_bias.shape, F32),
                vmem(tower_out.shape, BF16),
                vmem(tower_out_bias.shape, F32),
                vmem((rows, width), BF16),
                vmem((min(128, rows), out_w), F32),
                vmem((ranks, own, out_w), BF16),
                vmem((ranks, own, out_w), BF16),
                vmem((tasks, experts, own, 128), F32),
                vmem((plane_devs, tasks, own, out_w), BF16),
                vmem((tasks, plane_devs, own, out_w), F32),
                vmem((tasks, plane_devs, own, out_w), BF16),
                vmem((tasks, plane_devs, own, out_w), BF16),
                dma((13,)),
                dma((plane_devs,)),
                dma((plane_devs,)),
                dma((chips,)),
                dma((chips, tile_size)),
                dma((ranks,)),
                dma((ranks,)),
                dma((ranks,)),
                dma((tasks, plane_devs)),
                dma((tasks, plane_devs)),
                dma((tasks, plane_devs)),
                dma((tasks, plane_devs)),
            ],
            compiler_params=pltpu.CompilerParams(
                collective_id=0, has_side_effects=True, vmem_limit_bytes=60 * 1024 * 1024
            ),
        )(
            features, cross_weight, cross_bias.reshape(1, -1), gate_weight, unit_experts,
            up_weight, up_bias.reshape(1, -1), down_weight, down_bias, task_counts, tower_in,
            tower_in_bias, tower_out, tower_out_bias,
        )
        return jnp.transpose(result, (1, 0, 2))

    return jax.shard_map(
        body,
        mesh=mesh,
        in_specs=(
            P(("groups", "expert", "dp", "tile"), None),
            P(None, ("dp", "tile")),
            P(),
            P(),
            P(),
            P(None, ("expert", "dp")),
            P(("expert", "dp")),
            P(("expert", "dp"), None),
            P(),
            P(("groups", "expert", "dp", "tile"), None),
            P(None, None, ("dp", "tile")),
            P(None, ("dp", "tile")),
            P(None, ("dp", "tile"), None),
            P(),
        ),
        out_specs=P(("groups", "expert", "dp", "tile"), None, None),
        check_vma=False,
    )
```

time: 129 us -> 37.9 us (0.29)
  waiting for transfers between devices: 52.3 us -> 0 us
  blocking collectives: 36.2 us -> 0 us
  Pallas kernels: 0 us -> 34.5 us
  matrix products: 18 us -> 0 us
  between operations: 13.5 us -> 0.01 us
  starting transfers between devices: 4.57 us -> 0 us
  other arithmetic: 3.11 us -> 0 us
  local copies, waits for them, and re-layouts: 0.86 us -> 3.17 us
    all_gather x2 -> x0, blocking collectives: 36.2 us -> none  [the longest x1 30.6 us: body(): row_piece = lax.all_gather(crossed, ('expert', 'dp'), axis=0, tiled=True)]
    pallas_call x0 -> x1, Pallas kernels: none -> 34.5 us  [body(): pl.pallas_call(functools.partial(kernel, (planes, dp_size, tile_size)), o...]
    all_gather x1 -> x0, waiting for transfers between devices: 25.9 us -> none  [body(): lax.all_gather(cross_weight, ('dp', 'tile'), axis=1, tiled=True)]
    reduce_scatter x1 -> x0, waiting for transfers between devices: 19.2 us -> none  [body(): lax.psum_scatter(jnp.einsum('rth,tho->rto', hidden, tower_out, preferred_...]
    dot_general x7 -> x0, matrix products: 18 us -> none  [the longest x1 8.94 us: body(): jnp.dot(row_piece, up_weight, preferred_element_type=jnp.float32) + up_bias]
    all_to_all x1 -> x0, waiting for transfers between devices: 6.55 us -> none  [body(): lax.all_to_all(blocks, ('expert', 'dp'), split_axis=0, concat_axis=0, til...]
    all_to_all x1 -> x0, starting transfers between devices: 4.53 us -> none  [body(): lax.all_to_all(blocks, ('expert', 'dp'), split_axis=0, concat_axis=0, til...]
    unnamed x16 -> x2, local copies, waits for them, and re-layouts: 0.04 us -> 3.17 us
  transfers between devices with their start and end apart: 3 -> 0, of which waited for: 3 -> 0; matrix products, arithmetic and copies ran while one was open for 2% -> 0% of each run, Pallas kernels for 0% -> 0%
where the time goes in v1:
time: 37.9 us; the launch traced here: 37.7 us
  Pallas kernels  34.5 us (91%)
  local copies, waits for them, and re-layouts  3.17 us (8%)
    pallas_call x1, Pallas kernels, body(): pl.pallas_call(functools.partial(kernel, (planes, dp_size, tile_size)), o...  34.5 us
    unnamed x2, local copies, waits for them, and re-layouts  3.17 us

profile of v1, /device:TPU:0, one launch (start us, length us, event | category | flops | bytes accessed | tf_op | source)
XLA Modules:
  0.0 37.7 jit_solution(4997296685102986130)
XLA Ops:
  0.0 1.7 %copy.15.gate_weight = bf16[1024,36]{1,0:T(8,128)(2,1)} copy(bf16[1024,36]{0,1:T(8,128)(2,1)} %param.17) | data formatting | bytes 147456 | tf_op args[3]
  1.7 34.5 %shard_map.136 = bf16[6,8,512]{2,1,0:T(8,128)(2,1)} custom-call(bf16[8,1024]{1,0:T(8,128)(2,1)} %features.1, bf16[1024,256]{1,0:T(8,128)(2,1)} %cross_weight.1, f32[1,1024]{1,0:T(1,128)} %bitcast.5, bf16[1024,36]{1,0:T(8,128)(2,1)} %copy.15.gate_weight, s32[6,6]{1,0:T(8,128)} %unit_experts.1, bf16[1024,8192]{1,0:T(8,128)(2,1)} %up_weight.1, ...), custom_call_target="tpu_custom_call" | custom-call | tf_op jit(solution)/shard_map/pallas_call | solution.py:367
  36.2 1.4 %copy.17 = bf16[8,6,512]{2,0,1:T(8,128)(2,1)} copy(bf16[8,6,512]{2,0,1:T(8,128)(2,1)} %bitcast.3) | data formatting | bytes 98304
